TPU v7x, 256 devices: a whole 4x4x8 slice. The times are simulated.
256 devices in a mesh: dp: 16 (over x_lo, y, core), mp: 8 (over z), side: 2 (over x_hi).
Axes of the slice: x: 4 (x_hi: 2, x_lo: 2; x = x_hi * 2 + x_lo), y: 4, z: 8, core: 2. Of those that a mesh axis runs over, the one named last changes fastest.
Arguments:
- tokens: bfloat16 [4096, 3072], P('dp', 'mp'), may hold values from -6 to 6
- up_weight: bfloat16 [2, 3072, 6144], P('side', 'dp', 'mp'), may hold values from -0.109375 to 0.109375
- down_weight: bfloat16 [2, 6144, 3072], P('side', 'mp', 'dp'), may hold values from -0.078125 to 0.078125
- mod_table: float32 [2, 50, 3, 3072], P('side'), may hold values from -3 to 3
- timesteps: int32 [16], P('dp'), may hold values from 0 to 49
- valid_counts: int32 [16], replicated, may hold values from 64 to 256, as said below
Outputs:
- block_out: bfloat16 [2, 4096, 3072], P('side', 'dp', 'mp')
- up_grads: float32 [3072, 6144], P(('dp', 'side'), 'mp')
- down_grads: float32 [6144, 3072], P('mp', ('dp', 'side'))
Inputs may be any that keep to these rules, and one draw needn't show every extreme that they name: `valid_counts`: every image has at least 64 valid tokens, and in every draw some image has all 256 valid.
All inputs are finite; a program needn't handle non-finite values.
Results may differ from a plain program's by a relative error of at most 0.018.
Values may be sent and summed in bfloat16 or wider, within the bound.
A program may use at most 64 MiB of HBM per device.

v0:
```python
import jax
import jax.numpy as jnp
from jax import lax
from jax.sharding import PartitionSpec as P


def passed_along(x, axis, by):
    peers = lax.axis_size(axis)
    pairs = [(i, i + by) for i in range(peers) if 0 <= i + by < peers]
    return lax.ppermute(x, axis, pairs)


def gelu_tanh(values):
    return jax.nn.gelu(values, approximate=True)


def shards(tokens, up_weight, down_weight, mod_table, timesteps, valid_counts):
    gathered = lax.all_gather(tokens, "mp", axis=1, tiled=True)
    width = gathered.shape[1]
    shard_width = tokens.shape[1]
    mp_offset = lax.axis_index("mp") * shard_width
    is_student = lax.axis_index("side") == 1
    wide = gathered.astype(jnp.float32)
    average = jnp.mean(wide, axis=-1, keepdims=True)
    centred = wide - average
    variance = jnp.mean(centred * centred, axis=-1, keepdims=True)
    scaled = centred * lax.rsqrt(variance + 1e-06)
    plan = mod_table.shape[1]
    one_hot = (jnp.arange(plan, dtype=jnp.int32)[None, :] == timesteps[0]).astype(jnp.float32)
    modulation = jnp.dot(
        one_hot,
        mod_table[0].reshape(plan, 3 * width),
        precision=lax.Precision.HIGHEST,
        preferred_element_type=jnp.float32,
    ).reshape(3, width)
    normed = (scaled * (1.0 + modulation[1]) + modulation[0]).astype(jnp.bfloat16)
    gate_row = modulation[2]
    hidden_pre = jnp.dot(
        normed,
        lax.all_gather(up_weight[0], "dp", axis=0, tiled=True),
        preferred_element_type=jnp.float32,
    )
    hidden_act = gelu_tanh(hidden_pre).astype(jnp.bfloat16)
    down_full = lax.all_gather(down_weight[0], "dp", axis=1, tiled=True)
    partial_value = jnp.dot(hidden_act, down_full, preferred_element_type=jnp.float32)
    positions = jnp.arange(normed.shape[0], dtype=jnp.int32)
    own_count = lax.dynamic_index_in_dim(valid_counts, lax.axis_index("dp"), 0, keepdims=False)
    valid_col = (positions < own_count).astype(jnp.float32)[:, None]
    valid_total = jnp.sum(valid_counts).astype(jnp.float32)
    mixed = lax.psum(partial_value.astype(jnp.bfloat16), "mp").astype(jnp.float32)
    out_full = (wide + gate_row * mixed).astype(jnp.bfloat16)
    out_local = lax.dynamic_slice_in_dim(out_full, mp_offset, shard_width, 1)
    other_full = passed_along(out_full, "side", 1)
    differ = out_full.astype(jnp.float32) - other_full.astype(jnp.float32)
    grad_out = (gate_row * differ * valid_col / jnp.sqrt(valid_total)).astype(jnp.bfloat16)

    def backprop():
        grad_act = lax.dot_general(
            grad_out, down_full, (((1,), (1,)), ((), ())), preferred_element_type=jnp.float32
        )
        unused, pullback = jax.vjp(gelu_tanh, hidden_pre)
        return pullback(grad_act)[0].astype(jnp.bfloat16)

    def no_backprop():
        return jnp.zeros(hidden_pre.shape, jnp.bfloat16)

    grad_pre = lax.cond(is_student, backprop, no_backprop)
    ff_width = hidden_act.shape[1]

    def product():
        return lax.dot_general(
            normed, grad_pre, (((0,), (0,)), ((), ())), preferred_element_type=jnp.float32
        )

    def nothing():
        return jnp.zeros(
            (width // lax.axis_size(("dp", "side")) * lax.axis_size(("dp", "side")), ff_width),
            jnp.float32,
        )

    up_share = lax.psum_scatter(
        lax.cond(is_student, product, nothing).astype(jnp.bfloat16),
        ("dp", "side"),
        scatter_dimension=0,
        tiled=True,
    ).astype(jnp.float32)

    def down_product():
        return lax.dot_general(
            hidden_act, grad_out, (((0,), (0,)), ((), ())), preferred_element_type=jnp.float32
        )

    def down_nothing():
        return jnp.zeros((ff_width, width), jnp.float32)

    down_term = lax.cond(is_student, down_product, down_nothing)
    down_share = lax.psum_scatter(
        down_term.astype(jnp.bfloat16), ("dp", "side"), scatter_dimension=1, tiled=True
    ).astype(jnp.float32)
    return (out_local[None], up_share, down_share)


def solution(mesh):
    placed = (
        P("dp", "mp"),
        P("side", "dp", "mp"),
        P("side", "mp", "dp"),
        P("side", None, None, None),
        P("dp"),
        P(),
    )
    return jax.shard_map(
        shards,
        mesh=mesh,
        in_specs=placed,
        out_specs=(P("side", "dp", "mp"), P(("dp", "side"), "mp"), P("mp", ("dp", "side"))),
        check_vma=False,
    )
```

profile of v0, /device:TPU:1, one launch (start us, length us, event | category | flops | bytes accessed | tf_op | source)
XLA Modules:
  0.0 593.4 jit_solution(2284106600337096998)
XLA Ops:
  7.2 0.7 all-gather.6.cloned.1.call-update
  7.9 0.7 all-gather.8.cloned.1.call-update
  8.7 0.7 all-gather.10.cloned.1.call-update
  9.4 6.5 %reduce = f32[50,3,3072]{2,1,0:T(4,128)S(1)} reduce(f32[1,50,3,3072]{3,0,2,1:T(1,128)} %param.15, f32[]{:T(128)} %constant.65), dimensions={0}, to_apply=%param.15.reduce_sub_computation | reduce | bytes 3686404 | tf_op args[3]
  16.5 1.2 copy.14
  18.3 0.8 fusion.24
  19.1 29.2 %all-gather.6.cloned.1.call-done = bf16[256,3072]{1,0:T(8,128)(2,1)} async-done(((bf16[256,384]{1,0:T(8,128)(2,1)}), bf16[256,3072]{1,0:T(8,128)(2,1)}) %all-gather.6.cloned.1.call-update) | async-done | bytes 1572880 | tf_op jit(solution)/shard_map/all_gather | solution.py:18
  48.2 1.8 convert_reduce_fusion
  50.1 2.0 fusion.11
  52.0 0.8 fusion.14
  52.8 41.7 %all-gather.8.cloned.1.call-done = bf16[1,3072,768]{2,1,0:T(8,128)(2,1)} async-done(((bf16[1,192,768]{2,1,0:T(8,128)(2,1)}), bf16[1,3072,768]{2,1,0:T(8,128)(2,1)}) %all-gather.8.cloned.1.call-update) | async-done | bytes 4718608 | tf_op jit(solution)/shard_map/all_gather | solution.py:40
  94.5 4.6 fusion.23
  99.2 37.7 %all-gather.10.cloned.1.call-done = bf16[1,768,3072]{1,2,0:T(8,128)(2,1)} async-done(((bf16[1,768,192]{1,2,0:T(8,128)(2,1)}), bf16[1,768,3072]{1,2,0:T(8,128)(2,1)}) %all-gather.10.cloned.1.call-update) | async-done | bytes 4718608 | tf_op jit(solution)/shard_map/all_gather | solution.py:44
  136.9 4.9 convolution_convert_fusion
  142.1 74.3 %all-reduce.2.cloned.1.call-done = bf16[256,3072]{1,0:T(8,128)(2,1)} async-done(((bf16[256,3072]{1,0:T(8,128)(2,1)}), bf16[256,3072]{1,0:T(8,128)(2,1)}) %all-reduce.2.cloned.1.call-update) | async-done | bytes 1572880 | tf_op jit(solution)/shard_map/psum | solution.py:50
  216.3 3.1 fusion.15
  219.5 5.8 collective-permute-start
  225.2 0.6 reduce_sum.29
  227.2 0.6 compare_convert_fusion
  227.8 25.6 %collective-permute-done = bf16[256,3072]{1,0:T(8,128)(2,1)} collective-permute-done((bf16[256,3072]{1,0:T(8,128)(2,1)}, bf16[256,3072]{1,0:T(8,128)(2,1)}, u32[]{:S(2)}, u32[]{:S(2)}) %collective-permute-start) | collective-permute-done | bytes 1572896 | tf_op jit(solution)/shard_map/ppermute | solution.py:10
  253.4 2.6 divide_convert_fusion
  256.1 2.5 conditional.4
  256.1 2.5 broadcast.75
  258.6 0.9 copy-done.2
  259.6 2.8 conditional.5
  259.6 2.8 broadcast.76
  262.4 6.6 %copy.12 = bf16[768,3072]{0,1:T(8,128)(2,1)} copy(bf16[768,3072]{1,0:T(8,128)(2,1)} %get-tuple-element.43) | data formatting | bytes 9437184 | tf_op jit(solution)/shard_map/cond | solution.py:96
  269.0 1.6 dynamic-slice_bitcast_fusion
  270.6 155.2 %reduce-scatter.3.cloned.1.call-done = bf16[96,768]{1,0:T(8,128)(2,1)} async-done(((bf16[3072,768]{1,0:T(8,128)(2,1)}), bf16[96,768]{1,0:T(8,128)(2,1)}) %reduce-scatter.3.cloned.1.call-update) | async-done | bytes 147472 | tf_op jit(solution)/shard_map/reduce_scatter | solution.py:81
  425.9 1.6 convert_element_type.71
  427.5 157.4 %reduce-scatter.5.cloned.1.call-done = bf16[768,96]{0,1:T(8,128)(2,1)} async-done(((bf16[768,3072]{0,1:T(8,128)(2,1)}), bf16[768,96]{0,1:T(8,128)(2,1)}) %reduce-scatter.5.cloned.1.call-update) | async-done | bytes 147472 | tf_op jit(solution)/shard_map/reduce_scatter | solution.py:97
  584.9 1.6 convert_element_type.73
  (23 shorter events, 1.7 us)
Async XLA Ops:
  7.2 41.1 %all-gather.6.cloned.1.call-start = ((), (), s32[]{:S(2)}) async-start(), calls=%async_computation.2 | async-start | bytes 1769472 | tf_op jit(solution)/shard_map/all_gather | solution.py:18
  7.9 86.6 %all-gather.8.cloned.1.call-start = ((), (), s32[]{:S(2)}) async-start(), calls=%async_computation.6 | async-start | bytes 5013504 | tf_op jit(solution)/shard_map/all_gather | solution.py:40
  8.6 128.2 %all-gather.10.cloned.1.call-start = ((), (), s32[]{:S(2)}) async-start(), calls=%async_computation.7 | async-start | bytes 5013504 | tf_op jit(solution)/shard_map/all_gather | solution.py:44
  9.4 207.0 %all-reduce.2.cloned.1.call-start = ((), (), s32[]{:S(2)}) async-start(), calls=%async_computation.3 | async-start | bytes 3145728 | tf_op jit(solution)/shard_map/psum | solution.py:50
  48.2 3.8 copy-start
  99.2 42.7 %copy-start.1 = (bf16[256,768]{1,0:T(8,128)(2,1)}, bf16[256,768]{1,0:T(8,128)(2,1)S(1)}, u32[]{:S(2)}) copy-start(bf16[256,768]{1,0:T(8,128)(2,1)S(1)} %get-tuple-element.39) | copy-start | bytes 1179652
  141.8 83.4 %copy-start.3 = (s32[16]{0:T(128)S(1)}, s32[16]{0:T(128)}, u32[]{:S(2)}) copy-start(s32[16]{0:T(128)} %param.17) | copy-start | bytes 196
  141.8 284.0 %reduce-scatter.3.cloned.1.call-start = ((), (), s32[]{:S(2)}) async-start(), calls=%async_computation.4 | async-start | bytes 4866048 | tf_op jit(solution)/shard_map/reduce_scatter | solution.py:81
  219.5 34.0 %collective-permute-start = (bf16[256,3072]{1,0:T(8,128)(2,1)}, bf16[256,3072]{1,0:T(8,128)(2,1)}, u32[]{:S(2)}, u32[]{:S(2)}) collective-permute-start(bf16[256,3072]{1,0:T(8,128)(2,1)} %fusion.15), channel_id=1, source_target_pairs={{0,1},{2,3},{4,5},{6,7},{8,9},{10,11},{12,13},{14,15},{16,17},{18,... | collective-permute-start | bytes 4718600 | tf_op jit(solution)/shard_map/ppermute | solution.py:10
  258.6 1.0 copy-start.2
  258.6 326.3 %reduce-scatter.5.cloned.1.call-start = ((), (), s32[]{:S(2)}) async-start(), calls=%async_computation.5 | async-start | bytes 4866048 | tf_op jit(solution)/shard_map/reduce_scatter | solution.py:97
Sparse Core Ops, SparseCore 0:
  9.8 38.4 all-gather.5
  50.1 44.3 all-gather.7
  96.4 40.4 all-gather.9
  142.0 74.3 all-reduce.1
  258.7 167.0 reduce-scatter.2
  428.2 156.6 reduce-scatter.4
where the time goes:
time: 594 us; the launch traced here: 593 us
  waiting for transfers between devices  523 us (88%)
  other arithmetic  21.3 us (4%)
  local copies, waits for them, and re-layouts  16.8 us (3%)
  between operations  15.5 us (3%)
  matrix products  10.3 us (2%)
  starting transfers between devices  6.19 us (1%)
    reduce_scatter x1, waiting for transfers between devices, shards(): lax.psum_scatter(down_term.astype(jnp.bfloat16), ('dp', 'side'), scatter_...  157 us
    reduce_scatter x1, waiting for transfers between devices, shards(): lax.psum_scatter(lax.cond(is_student, product, nothing).astype(jnp.bfloat...  155 us
    psum x1, waiting for transfers between devices, shards(): lax.psum(partial_value.astype(jnp.bfloat16), 'mp').astype(jnp.float32)  74.3 us
    all_gather x1, waiting for transfers between devices, shards(): lax.all_gather(up_weight[0], 'dp', axis=0, tiled=True)  41.7 us
    all_gather x1, waiting for transfers between devices, shards(): down_full = lax.all_gather(down_weight[0], 'dp', axis=1, tiled=True)  37.7 us
    all_gather x1, waiting for transfers between devices, shards(): gathered = lax.all_gather(tokens, 'mp', axis=1, tiled=True)  29.2 us
    ppermute x1, waiting for transfers between devices, passed_along(): return lax.ppermute(x, axis, pairs)  25.6 us
  transfers between devices with their start and end apart: 7, of which 7 were waited for; matrix products, arithmetic and copies ran while one was open for 6% of the time, Pallas kernels for 0%

commit v1 on v0

--- a/solution.py
+++ b/solution.py
@@ -47,7 +47,9 @@
     own_count = lax.dynamic_index_in_dim(valid_counts, lax.axis_index("dp"), 0, keepdims=False)
     valid_col = (positions < own_count).astype(jnp.float32)[:, None]
     valid_total = jnp.sum(valid_counts).astype(jnp.float32)
-    mixed = lax.psum(partial_value.astype(jnp.bfloat16), "mp").astype(jnp.float32)
+    mixed = jnp.sum(lax.all_gather(partial_value.astype(jnp.bfloat16), "mp"), axis=0).astype(
+        jnp.float32
+    )
     out_full = (wide + gate_row * mixed).astype(jnp.bfloat16)
     out_local = lax.dynamic_slice_in_dim(out_full, mp_offset, shard_width, 1)
     other_full = passed_along(out_full, "side", 1)

time: 594 us -> 662 us (1.11)
  waiting for transfers between devices: 523 us -> 584 us
  other arithmetic: 21.3 us -> 30.2 us
    all_gather x0 -> x1, waiting for transfers between devices: none -> 133 us  [shards(): lax.all_gather(partial_value.astype(jnp.bfloat16), 'mp')]
    psum x1 -> x0, waiting for transfers between devices: 74.3 us -> none  [shards(): lax.psum(partial_value.astype(jnp.bfloat16), 'mp').astype(jnp.float32)]
    reduce_sum x0 -> x1, other arithmetic: none -> 8.76 us  [shards(): jnp.sum(lax.all_gather(partial_value.astype(jnp.bfloat16), 'mp'), axis=0)]
  transfers between devices with their start and end apart: 7 -> 7, of which waited for: 7 -> 7; matrix products, arithmetic and copies ran while one was open for 6% -> 4% of each run, Pallas kernels for 0% -> 0%
where the time goes in v1:
time: 662 us
  waiting for transfers between devices  584 us (88%)
  other arithmetic  30.2 us (5%)
  local copies, waits for them, and re-layouts  15.8 us (2%)
  between operations  15.5 us (2%)
  matrix products  10.3 us (2%)
    reduce_scatter x1, waiting for transfers between devices, shards(): lax.psum_scatter(lax.cond(is_student, product, nothing).astype(jnp.bfloat...  157 us
    reduce_scatter x1, waiting for transfers between devices, shards(): lax.psum_scatter(down_term.astype(jnp.bfloat16), ('dp', 'side'), scatter_...  154 us
    all_gather x1, waiting for transfers between devices, shards(): lax.all_gather(partial_value.astype(jnp.bfloat16), 'mp')  133 us
    all_gather x1, waiting for transfers between devices, shards(): lax.all_gather(up_weight[0], 'dp', axis=0, tiled=True)  41.7 us
    all_gather x1, waiting for transfers between devices, shards(): down_full = lax.all_gather(down_weight[0], 'dp', axis=1, tiled=True)  37.7 us
    ppermute x1, waiting for transfers between devices, passed_along(): return lax.ppermute(x, axis, pairs)  29.5 us
    all_gather x1, waiting for transfers between devices, shards(): gathered = lax.all_gather(tokens, 'mp', axis=1, tiled=True)  29.2 us
  transfers between devices with their start and end apart: 7, of which 7 were waited for; matrix products, arithmetic and copies ran while one was open for 4% of the time, Pallas kernels for 0%

profile of v1, /device:TPU:1, one launch (start us, length us, event | category | flops | bytes accessed | tf_op | source)
XLA Modules:
  0.0 661.6 jit_solution(3840718613388631985)
XLA Ops:
  7.2 0.7 all-gather.8.cloned.1.call-update
  7.9 0.7 all-gather.10.cloned.1.call-update
  8.7 0.7 all-gather.12.cloned.1.call-update
  9.4 6.5 reduce.1
  16.5 1.2 copy.14
  18.3 0.8 fusion.24
  19.1 29.2 %all-gather.8.cloned.1.call-done = bf16[256,3072]{1,0:T(8,128)(2,1)} async-done(((bf16[256,384]{1,0:T(8,128)(2,1)}), bf16[256,3072]{1,0:T(8,128)(2,1)}) %all-gather.8.cloned.1.call-update) | async-done | bytes 1572880 | tf_op jit(solution)/shard_map/all_gather | solution.py:18
  48.2 1.8 convert_reduce_fusion
  50.1 2.0 fusion.11
  52.0 0.8 fusion.14
  52.8 41.7 %all-gather.10.cloned.1.call-done = bf16[1,3072,768]{2,1,0:T(8,128)(2,1)} async-done(((bf16[1,192,768]{2,1,0:T(8,128)(2,1)}), bf16[1,3072,768]{2,1,0:T(8,128)(2,1)}) %all-gather.10.cloned.1.call-update) | async-done | bytes 4718608 | tf_op jit(solution)/shard_map/all_gather | solution.py:40
  94.5 4.6 fusion.23
  99.1 37.7 %all-gather.12.cloned.1.call-done = bf16[1,768,3072]{1,2,0:T(8,128)(2,1)} async-done(((bf16[1,768,192]{1,2,0:T(8,128)(2,1)}), bf16[1,768,3072]{1,2,0:T(8,128)(2,1)}) %all-gather.12.cloned.1.call-update) | async-done | bytes 4718608 | tf_op jit(solution)/shard_map/all_gather | solution.py:44
  136.9 4.9 convolution_convert_fusion
  142.1 132.8 %all-gather.14.cloned.1.call-done = bf16[2048,3072]{1,0:T(8,128)(2,1)} async-done(((bf16[256,3072]{1,0:T(8,128)(2,1)}), bf16[2048,3072]{1,0:T(8,128)(2,1)}) %all-gather.14.cloned.1.call-update) | async-done | bytes 12582928 | tf_op jit(solution)/shard_map/all_gather | solution.py:50
  274.9 8.8 %reduce_sum.41 = bf16[256,3072]{1,0:T(8,128)(2,1)} reduce(bf16[8,256,3072]{2,1,0:T(8,128)(2,1)} %bitcast.31, bf16[]{:T(256)} %constant.53.clone.1), dimensions={0}, to_apply=%region_2.3 | reduce | flops 5505024 | bytes 14155778 | tf_op jit(solution)/shard_map/reduce_sum | solution.py:50
  283.6 3.2 fusion.15
  286.8 5.7 collective-permute-start
  292.6 0.6 reduce_sum.42
  294.5 0.7 compare_convert_fusion
  295.1 29.5 %collective-permute-done = bf16[256,3072]{1,0:T(8,128)(2,1)} collective-permute-done((bf16[256,3072]{1,0:T(8,128)(2,1)}, bf16[256,3072]{1,0:T(8,128)(2,1)}, u32[]{:S(2)}, u32[]{:S(2)}) %collective-permute-start) | collective-permute-done | bytes 1572896 | tf_op jit(solution)/shard_map/ppermute | solution.py:10
  324.6 2.6 divide_convert_fusion
  327.2 2.8 conditional.5
  327.2 2.8 broadcast.76
  330.0 6.6 %copy.12 = bf16[768,3072]{0,1:T(8,128)(2,1)} copy(bf16[768,3072]{1,0:T(8,128)(2,1)} %get-tuple-element.43) | data formatting | bytes 9437184 | tf_op jit(solution)/shard_map/cond | solution.py:98
  336.8 2.5 conditional.4
  336.8 2.5 broadcast.75
  339.3 1.6 dynamic-slice_bitcast_fusion
  340.9 153.5 %reduce-scatter.5.cloned.1.call-done = bf16[768,96]{0,1:T(8,128)(2,1)} async-done(((bf16[768,3072]{0,1:T(8,128)(2,1)}), bf16[768,96]{0,1:T(8,128)(2,1)}) %reduce-scatter.5.cloned.1.call-update) | async-done | bytes 147472 | tf_op jit(solution)/shard_map/reduce_scatter | solution.py:99
  494.4 1.6 convert_element_type.75
  496.1 157.0 %reduce-scatter.3.cloned.1.call-done = bf16[96,768]{1,0:T(8,128)(2,1)} async-done(((bf16[3072,768]{1,0:T(8,128)(2,1)}), bf16[96,768]{1,0:T(8,128)(2,1)}) %reduce-scatter.3.cloned.1.call-update) | async-done | bytes 147472 | tf_op jit(solution)/shard_map/reduce_scatter | solution.py:83
  653.1 1.6 convert_element_type.73
  (20 shorter events, 1.7 us)
Async XLA Ops:
  7.2 41.1 %all-gather.8.cloned.1.call-start = ((), (), s32[]{:S(2)}) async-start(), calls=%async_computation.2 | async-start | bytes 1769472 | tf_op jit(solution)/shard_map/all_gather | solution.py:18
  7.9 86.6 %all-gather.10.cloned.1.call-start = ((), (), s32[]{:S(2)}) async-start(), calls=%async_computation.5 | async-start | bytes 5013504 | tf_op jit(solution)/shard_map/all_gather | solution.py:40
  8.6 128.2 %all-gather.12.cloned.1.call-start = ((), (), s32[]{:S(2)}) async-start(), calls=%async_computation.6 | async-start | bytes 5013504 | tf_op jit(solution)/shard_map/all_gather | solution.py:44
  9.4 265.5 %all-gather.14.cloned.1.call-start = ((), (), s32[]{:S(2)}) async-start(), calls=%async_computation.7 | async-start | bytes 14155776 | tf_op jit(solution)/shard_map/all_gather | solution.py:50
  48.2 3.8 copy-start
  141.9 352.6 %reduce-scatter.5.cloned.1.call-start = ((), (), s32[]{:S(2)}) async-start(), calls=%async_computation.4 | async-start | bytes 4866048 | tf_op jit(solution)/shard_map/reduce_scatter | solution.py:99
  283.6 8.9 %copy-start.1 = (s32[16]{0:T(128)S(1)}, s32[16]{0:T(128)}, u32[]{:S(2)}) copy-start(s32[16]{0:T(128)} %param.17) | copy-start | bytes 196
  286.8 37.8 %collective-permute-start = (bf16[256,3072]{1,0:T(8,128)(2,1)}, bf16[256,3072]{1,0:T(8,128)(2,1)}, u32[]{:S(2)}, u32[]{:S(2)}) collective-permute-start(bf16[256,3072]{1,0:T(8,128)(2,1)} %fusion.15), channel_id=1, source_target_pairs={{0,1},{2,3},{4,5},{6,7},{8,9},{10,11},{12,13},{14,15},{16,17},{18,... | collective-permute-start | bytes 4718600 | tf_op jit(solution)/shard_map/ppermute | solution.py:10
  336.7 316.4 %reduce-scatter.3.cloned.1.call-start = ((), (), s32[]{:S(2)}) async-start(), calls=%async_computation.3 | async-start | bytes 4866048 | tf_op jit(solution)/shard_map/reduce_scatter | solution.py:83
Sparse Core Ops, SparseCore 0:
  9.8 38.4 all-gather.7
  50.1 44.3 all-gather.9
  96.4 40.4 all-gather.11
  142.0 132.8 all-gather.13
  336.8 157.5 reduce-scatter.4
  496.8 156.2 reduce-scatter.2
